TPU v7x, 32 devices: a whole 2x2x4 slice. The times are simulated.
32 devices in a mesh: avg: 4 (over x, core), space: 8 (over z, y).
Axes of the slice: x: 2, y: 2, z: 4, core: 2. Of those that a mesh axis runs over, the one named last changes fastest.
Arguments:
- spectral_state: float32 [3, 2, 1024, 1024], P(None, None, 'space', 'avg'), may hold values from -6 to 6
- phase_index: int32 [4], P('avg'), may hold values from 0 to 63
- weight_count: int32 [4], P('avg'), may hold values from 1 to 7
Outputs:
- advanced: float32 [3, 2, 1024, 1024], P(None, None, 'space', 'avg')
All inputs are finite; a program needn't handle non-finite values.
Results may differ from a plain program's by a relative error of at most 0.015.
Values may be sent and summed in bfloat16 or wider, within the bound.
A program may use at most 64 MiB of HBM per device.

v0:
```python
import functools

import jax
import jax.numpy as jnp
import ml_dtypes
import numpy as np
from jax import lax
from jax.experimental import pallas as pl
from jax.experimental.pallas import tpu as pltpu
from jax.sharding import PartitionSpec as P

coriolis = 1.0
wave_speed = 6.0
phase_step = 0.25
time_step = 2.0
weight_scale = 4.0


def wave_of(positions, length):
    shifted = (positions + length // 2) % length - length // 2
    return shifted.astype(jnp.float32) * (2.0 / length)


def circle(products, length):
    angles = (products % length) * (2.0 * np.pi / length)
    return np.cos(angles).astype(np.float32), np.sin(angles).astype(np.float32)


def slot_base(slot, slots, half):
    return np.where(slot < slots // 2, 2 * half * slot, 2 * half * (slots - 1 - slot) + half)


def packed_table(length, slots, chunks):
    half = length // (2 * slots)
    rows = slot_base(np.arange(slots), slots, half)[:, None] + np.arange(half)
    cosine, sine = circle(rows[:, :, None] * np.arange(length), length)
    packed = np.stack([cosine, -sine], axis=1)
    packed[0, 1, 0] = circle(length // 2 * np.arange(length), length)[0]
    packed = packed.reshape(slots, 2, chunks, half // chunks, length).transpose(2, 0, 1, 3, 4)
    return packed.reshape(length, length).astype(ml_dtypes.bfloat16)


def turned(first, second):
    (c, s), (d, t) = first, second
    return c * d - s * t, s * d + c * t


def angle_tables(length, width, owners):
    y = np.arange(length)
    return [
        jnp.asarray(np.stack(circle(step * np.arange(count)[:, None] * y, length)))
        for step, count in ((width, owners), (FINE, width // FINE), (1, FINE))
    ]


def wave_operator(fields, kx, ky):
    (er, ei), (nr, ni), (hr, hi) = fields
    cx, cy = wave_speed * kx, wave_speed * ky
    return (
        (coriolis * nr + cx * hi, coriolis * ni - cx * hr),
        (cy * hi - coriolis * er, -coriolis * ei - cy * hr),
        (cx * ei + cy * ni, -(cx * er + cy * nr)),
    )


def wave_factors(kx, ky, phase):
    square = coriolis * coriolis + wave_speed * wave_speed * (kx * kx + ky * ky)
    frequency = jnp.sqrt(square)
    angle = frequency * phase
    return jnp.sin(angle) / frequency, (1.0 - jnp.cos(angle)) / square


def wave_exponential(fields, kx, ky, factors):
    sine, cosine = factors
    single = wave_operator(fields, kx, ky)
    double = wave_operator(single, kx, ky)
    return tuple(
        tuple(w + sine * a + cosine * b for w, a, b in zip(ws, one, two))
        for ws, one, two in zip(fields, single, double)
    )


def planes(fields):
    return tuple((fields[i, 0], fields[i, 1]) for i in range(fields.shape[0]))


MESH = pl.DeviceIdType.MESH
EDGE = 16
FINE = 16


def column(info, t, index):
    return info[t, :, index : index + 1]


def positions():
    g, a = lax.axis_index("space"), lax.axis_index("avg")
    return g, a, a // 2, a % 2


def edge_partner(g, slots):
    aligned = 1 - (g % (slots // 2) + slots // 2 - 1) // (slots // 2)
    return ((slots - g) % slots + aligned * (slots // 2)) % slots


def greet(slots, chips, edges):
    g, a, q, core = positions()
    barrier = pltpu.get_barrier_semaphore()
    peers = [((g + d) % slots, a) for d in range(1, slots)]
    peers += [(g, 2 * q + 1 - core)]
    peers += [(g, 2 * ((q + m) % chips) + core) for m in range(1, chips)]
    if edges:
        across = edge_partner(g, slots)
        peers += [
            (across, 2 * ((q + m) % chips) + (core + c) % 2)
            for c in range(2) for m in range(chips) if c or m
        ]
    for space, avg in peers:
        pl.semaphore_signal(
            barrier, inc=1, device_id={"space": space, "avg": avg}, device_id_type=MESH
        )
    pl.semaphore_wait(barrier, len(peers))


def sending(slots):
    return sorted(range(1, slots), key=lambda d: (-min(d, slots - d), d))


def remote(src, dst, send, recv, space, avg):
    return pltpu.make_async_remote_copy(
        src_ref=src, dst_ref=dst, send_sem=send, recv_sem=recv,
        device_id={"space": space, "avg": avg}, device_id_type=MESH,
    )


DIMS_NT = (((1,), (1,)), ((), ()))


def step_kernel(
    dims, state, into_rows, back_rows, info, ky, own_kx, phase, blocks, steps, fines, packed_hbm, result,
    moved, top, gx, eg, rows_c, rows_s, half, arr, arr_t, grid, products, packed, ct, st, sine, cosine,
    end_sine, end_cosine, fh, ret, lhs, stage, rsin, acc, xs, rx, fin, own, other, edge,
    ex_s, ex_r, eg_s, eg_r, x_s, x_r, c_s, c_r, a_s, a_r, l_s,
    b_s, b_r, m_s, d_s, d_r, y_s, y_r, gv_s, gv_r, le_s, le_r, bring_s,
):
    slots, chips, chunks, hb, width, block = dims
    length, reach = slots * block, block // 2
    g, a, q, core = positions()
    low, high = g < slots // 2, g >= slots // 2
    partner = 2 * q + 1 - core
    across = edge_partner(g, slots)
    side = g // (slots // 2)
    bring = pltpu.make_async_copy(packed_hbm, packed, bring_s)

    for f in range(3):
        for i in range(2):
            plane = state[f, i].astype(jnp.bfloat16)
            top[f, i] = plane[:EDGE]
            picked = jnp.dot(into_rows[side], plane, preferred_element_type=jnp.float32)
            picked = picked.astype(jnp.bfloat16)
            for s in range(2):
                for t in range(chunks):
                    spot = s * reach + t * hb
                    moved[s, t, f, i] = picked[spot : spot + hb]
    greet(slots, chips, True)

    def build_factors(unused):
        for t in range(chunks):
            for s in range(2):
                def one(j, carry, t=t, s=s):
                    span = pl.ds(pl.multiple_of(j * 256, 256), 256)
                    factors = wave_factors(column(info, t, s), ky[:, span], phase[...])
                    sine[t, s, :, span], cosine[t, s, :, span] = factors
                    return carry
                lax.fori_loop(0, length // 256, one, 0)

    def own_factors():
        end_sine[...], end_cosine[...] = wave_factors(own_kx[...], ky[:, :width], time_step)

    def build_tables():
        for c in range(2):
            for m in range(chips):
                owner = 2 * ((q + m) % chips) + (core + c) % 2
                first = (blocks[0, pl.ds(owner, 1), :], blocks[1, pl.ds(owner, 1), :])

                def one(h, carry, j=c * chips + m, first=first):
                    begin = turned(first, (steps[0, pl.ds(h, 1), :], steps[1, pl.ds(h, 1), :]))
                    cos_rows, sin_rows = turned(begin, (fines[0], fines[1]))
                    at = pl.ds(pl.multiple_of(j * width + h * FINE, FINE), FINE)
                    ct[at, :] = cos_rows.astype(jnp.bfloat16)
                    st[at, :] = sin_rows.astype(jnp.bfloat16)
                    return carry
                lax.fori_loop(0, width // FINE, one, 0)

    exchange = [
        remote(moved.at[1, t], gx.at[t, 1, 0, 0], ex_s.at[t], ex_r.at[t], slots - 1 - g, a)
        for t in range(chunks)
    ]
    edges = [
        remote(top, eg.at[c, m], eg_s.at[c, m], eg_r.at[c, m],
               across, 2 * ((q + chips - m) % chips) + (core + c) % 2)
        for c in range(2) for m in range(chips)
    ]

    def mine(t, s):
        return gx.at[t, 1, 0, 0] if s else moved.at[0, t]

    def over_chips(t, s, m):
        return remote(mine(t, s), gx.at[t, s, 0, m], x_s.at[t, s, m], x_r.at[t, s, m],
                      g, 2 * ((q + chips - m) % chips) + core)

    def over_cores(t, s, m):
        source = gx.at[t, s, 0, m] if m else mine(t, s)
        return remote(source, gx.at[t, s, 1, m], c_s.at[t, s, m], c_r.at[t, s, m], g, partner)

    def to_grid(t, d):
        to = (g + d) % slots
        return remote(half.at[t, to], arr.at[t, g], a_s.at[t, d], a_r.at[t, d], to, a)

    exchange[0].start()

    @pl.when(high)
    def _():
        for copy in edges:
            copy.start()
        eg[...] = jnp.zeros_like(eg)

    for t in range(1, chunks):
        exchange[t].start()
    for t in range(chunks):
        for m in range(1, chips):
            over_chips(t, 0, m).start()
        over_cores(t, 0, 0).start()
    bring.start()
    build_factors(0)
    build_tables()
    for t in range(chunks):
        for m in range(1, chips):
            over_chips(t, 0, m).wait_recv()
            over_cores(t, 0, m).start()
    def spread(t):
        exchange[t].wait_recv()
        for m in range(1, chips):
            over_chips(t, 1, m).start()
        over_cores(t, 1, 0).start()

    spread(0)
    for t in range(chunks):
        for m in range(1, chips):
            over_chips(t, 1, m).wait_recv()
            over_cores(t, 1, m).start()
        if t + 1 < chunks:
            spread(t + 1)
        if t == 0:
            @pl.when(low)
            def _():
                for copy in edges:
                    copy.wait_recv()
        for s in range(2):
            for m in range(chips):
                over_cores(t, s, m).wait_recv()
        own_pair = column(info, t, 2) > 0.5
        sign = column(info, t, 3)
        for j in range(2 * chips):
            c, m = divmod(j, chips)
            span = slice(j * width, (j + 1) * width)
            turned_rows = []
            for s in range(2):
                source = moved.at[0, t] if s + j == 0 else gx.at[t, s, c, m]
                fields = [[source[f, i].astype(jnp.float32) for i in range(2)] for f in range(3)]
                if s == 1 and t == 0:
                    put = column(info, t, 4)[:EDGE] > 0.5
                    for f in range(3):
                        for i in range(2):
                            top = jnp.where(put, eg[c, m, f, i].astype(jnp.float32), fields[f][i][:EDGE])
                            fields[f][i] = (
                                jnp.concatenate([top, fields[f][i][EDGE:]], axis=0) if hb > EDGE else top
                            )
                turned_rows.append(wave_exponential(
                    fields, column(info, t, s), ky[:, span], (sine[t, s, :, span], cosine[t, s, :, span])
                ))
            for f in range(3):
                (re0, im0), (re1, im1) = turned_rows[0][f], turned_rows[1][f]
                for i, value in enumerate((
                    jnp.where(own_pair, re0, re0 + re1), jnp.where(own_pair, re1, sign * (im0 - im1))
                )):
                    rows_c[(i * 3 + f) * hb : (i * 3 + f + 1) * hb, span] = value.astype(jnp.bfloat16)
                for i, value in enumerate((
                    jnp.where(own_pair, -im0, -(im0 + im1)), jnp.where(own_pair, -im1, sign * (re0 - re1))
                )):
                    rows_s[(i * 3 + f) * hb : (i * 3 + f + 1) * hb, span] = value.astype(jnp.bfloat16)
        tile = min(length, max(block, 256))
        for y in range(0, length, tile):
            value = (
                jnp.dot(rows_c[...], ct[:, y : y + tile], preferred_element_type=jnp.float32)
                + jnp.dot(rows_s[...], st[:, y : y + tile], preferred_element_type=jnp.float32)
            ).astype(jnp.bfloat16)
            for b in range(tile // block):
                for i in range(2):
                    for f in range(3):
                        half[t, y // block + b, i * hb : (i + 1) * hb, f * block : (f + 1) * block] = (
                            value[(i * 3 + f) * hb : (i * 3 + f + 1) * hb, b * block : (b + 1) * block]
                        )
        for d in sending(slots):
            to_grid(t, d).start()
        pltpu.make_async_copy(half.at[t, g], arr.at[t, g], l_s.at[t]).start()
    def to_rows(t, d):
        to = (g + d) % slots
        return remote(fh.at[t, to], ret.at[t, g], b_s.at[t, d], b_r.at[t, d], to, a)

    def sum_cores(t):
        return remote(stage.at[t, 1], rsin.at[t], d_s.at[t], d_r.at[t], g, partner)

    def sum_chips(t, m):
        return remote(xs.at[t, m], rx.at[t, m], y_s.at[t, m], y_r.at[t, m],
                      g, 2 * ((q + m) % chips) + core)

    def give(t):
        return remote(fin.at[t], other.at[t], gv_s.at[t], gv_r.at[t], slots - 1 - g, a)

    last = remote(fin.at[0, :, :, :EDGE], edge, le_s, le_r, edge_partner(g, slots), a)

    bring.wait()
    for t in range(chunks):
        for d in range(1, slots):
            to_grid(t, d).wait_recv()
        pltpu.make_async_copy(half.at[t, g], arr.at[t, g], l_s.at[t]).wait()
        together = max(1, 128 // (2 * hb))
        for p in range(0, slots, together):
            value = arr[t, p : p + together].astype(jnp.float32)
            value = value.reshape(together * 2 * hb, 3 * block)
            spot = p * 2 * hb
            arr_t[:, spot : spot + together * 2 * hb] = value.T.astype(jnp.bfloat16)
        depth = length // chunks
        for x in range(0, length, 256):
            value = jnp.dot(
                arr_t[...], packed[t * depth : (t + 1) * depth, x : x + 256],
                preferred_element_type=jnp.float32,
            )
            if t:
                value = value + grid[:, x : x + 256]
            if t < chunks - 1:
                grid[:, x : x + 256] = value
            else:
                value = value * (1.0 / length)
                east, north, height = (value[i * block : (i + 1) * block] for i in range(3))
                for k, pair in enumerate((
                    east * east, east * north, north * north, east * height, north * height
                )):
                    products[k * block : (k + 1) * block, x : x + 256] = pair.astype(jnp.bfloat16)
    for t in range(chunks):
        for k in range(0, depth, 256):
            value = lax.dot_general(
                packed[t * depth + k : t * depth + k + 256, :], products[...], DIMS_NT,
                preferred_element_type=jnp.float32,
            ).astype(jnp.bfloat16)
            for n in range(256 // (2 * hb)):
                fh[t, k // (2 * hb) + n] = value[n * 2 * hb : (n + 1) * 2 * hb]
        for d in sending(slots):
            to_rows(t, d).start()
        pltpu.make_async_copy(fh.at[t, g], ret.at[t, g], m_s.at[t]).start()
    own_factors()

    @pl.when(low)
    def _():
        edge[...] = jnp.zeros_like(edge)

    def finish(t):
        for m in range(1, chips):
            sum_chips(t, m).wait_recv()
            acc[...] += rx[t, m].astype(jnp.float32)
        fin[t] = acc[1].astype(jnp.bfloat16)
        give(t).start()
        if t == 0:
            @pl.when(low)
            def _():
                last.start()
        own[t] = acc[0].astype(jnp.bfloat16)

    for t in range(chunks):
        for d in range(1, slots):
            to_rows(t, d).wait_recv()
        pltpu.make_async_copy(fh.at[t, g], ret.at[t, g], m_s.at[t]).wait()
        for p in range(slots):
            for k in range(5):
                lhs[k * 2 * hb : (k + 1) * 2 * hb, p * block : (p + 1) * block] = (
                    ret[t, p, :, k * block : (k + 1) * block]
                )
        own_pair = column(info, t, 2) > 0.5
        sign, scale = column(info, t, 3), column(info, t, 5)
        for j in range(2 * chips):
            c, m = divmod(j, chips)
            span = slice(j * width, (j + 1) * width)
            by_c = lax.dot_general(lhs[...], ct[span, :], DIMS_NT, preferred_element_type=jnp.float32)
            by_s = lax.dot_general(lhs[...], st[span, :], DIMS_NT, preferred_element_type=jnp.float32)

            def part(values, k, i):
                return values[(2 * k + i) * hb : (2 * k + i + 1) * hb]

            for s in range(2):
                turn = scale * sign if s == 0 else -scale * sign
                real, imag = [], []
                for k in range(5):
                    rc, ic = part(by_c, k, 0), part(by_c, k, 1)
                    rs, iz = part(by_s, k, 0), part(by_s, k, 1)
                    real.append(jnp.where(own_pair, scale * (ic if s else rc), scale * rc + turn * iz))
                    imag.append(jnp.where(own_pair, -scale * (iz if s else rs), turn * ic - scale * rs))
                kx, kyj = column(info, t, s), ky[:, span]
                tendency = [
                    (kx * imag[u] + kyj * imag[v], -(kx * real[u] + kyj * real[v]))
                    for u, v in ((0, 1), (1, 2), (3, 4))
                ]
                back = wave_exponential(
                    tendency, kx, kyj, (-sine[t, s, :, span], cosine[t, s, :, span])
                )
                for f in range(3):
                    for i in range(2):
                        stage[t, c, m, s, f, i] = back[f][i].astype(jnp.bfloat16)
        sum_cores(t).start()
        if t:
            finish(t - 1)
        sum_cores(t).wait_recv()
        for m in range(1, chips):
            xs[t, m] = (
                stage[t, 0, m].astype(jnp.float32) + rsin[t, m].astype(jnp.float32)
            ).astype(jnp.bfloat16)
            sum_chips(t, m).start()
        acc[...] = stage[t, 0, 0].astype(jnp.float32) + rsin[t, 0].astype(jnp.float32)
    finish(chunks - 1)
    for t in range(chunks):
        give(t).wait_recv()

    @pl.when(high)
    def _():
        last.wait_recv()

    for t in range(chunks):
        exchange[t].wait_send()
        for s in range(2):
            for m in range(1, chips):
                over_chips(t, s, m).wait_send()
            for m in range(chips):
                over_cores(t, s, m).wait_send()
        for d in range(1, slots):
            to_grid(t, d).wait_send()

    @pl.when(high)
    def _():
        for copy in edges:
            copy.wait_send()


    for t in range(chunks):
        for d in range(1, slots):
            to_rows(t, d).wait_send()
        sum_cores(t).wait_send()
        for m in range(1, chips):
            sum_chips(t, m).wait_send()
        give(t).wait_send()

    @pl.when(low)
    def _():
        last.wait_send()


    for f in range(3):
        for i in range(2):
            rows = jnp.concatenate(
                [own[t, f, i] for t in range(chunks)] + [other[t, f, i] for t in range(chunks)]
                + [edge[f, i]], axis=0,
            )
            averaged = jnp.dot(back_rows[side], rows, preferred_element_type=jnp.float32)
            result[f, i] = state[f, i] + time_step * averaged
    fields = [[result[f, i] for i in range(2)] for f in range(3)]
    advanced = wave_exponential(fields, own_kx[...], ky[:, :width], (end_sine[...], end_cosine[...]))
    for f in range(3):
        for i in range(2):
            result[f, i] = advanced[f][i]


VMEM = pl.BlockSpec(memory_space=pltpu.VMEM)


def per_device(spectral_state, phase_index, weight_count):
    slots, owners = lax.axis_size("space"), lax.axis_size("avg")
    block, width = spectral_state.shape[2:]
    length, half = block * slots, block // 2
    chips = owners // 2
    chunks = max(1, half // CHUNK_ROWS)
    hb = half // chunks
    dims = (slots, chips, chunks, hb, width, block)
    g, a = lax.axis_index("space"), lax.axis_index("avg")
    q, core = a // 2, a % 2
    low = g < slots // 2
    phase = phase_index[0].astype(jnp.float32) * phase_step
    weight = weight_count[0].astype(jnp.float32) / (weight_scale * owners)

    m, c = jnp.arange(chips, dtype=jnp.int32), jnp.arange(2, dtype=jnp.int32)[:, None]
    order = (2 * ((q + m) % chips) + (core + c) % 2).reshape(-1)
    columns = (order[:, None] * width + jnp.arange(width, dtype=jnp.int32)).reshape(1, -1)
    ky = wave_of(columns, length)
    packed = jnp.asarray(packed_table(length, slots, chunks))

    base = jnp.where(low, 2 * half * g, 2 * half * (slots - 1 - g) + half)
    direct = base + jnp.arange(half, dtype=jnp.int32)
    mirror = jnp.where(direct == 0, length // 2, length - direct)
    first = wave_of(jnp.where(low, direct, mirror), length)
    second = wave_of(jnp.where(low, mirror, direct), length)
    ones = jnp.ones((half,), jnp.float32)
    start = (jnp.arange(half) == 0) & low
    info = jnp.stack([
        first, second, (direct == 0).astype(jnp.float32), jnp.where(low, ones, -ones),
        start.astype(jnp.float32), ones * (weight / length), ones, ones,
    ], axis=1).reshape(chunks, hb, 8)
    own_kx = wave_of(g * block + jnp.arange(block, dtype=jnp.int32)[:, None], length)

    r = np.arange(half)
    into = np.zeros((2, 2, half, block), np.float32)
    into[0, 0, r, r] = 1
    into[0, 1, r, half + r] = 1
    into[1, 0, r, half - r] = 1
    into[1, 1, r[1:], block - r[1:]] = 1
    into = jnp.asarray(into.reshape(2, block, block).astype(ml_dtypes.bfloat16))
    back = np.zeros((2, block, 2 * half + EDGE), np.float32)
    back[0, r, r] = 1
    back[0, half + r, half + r] = 1
    back[1, half - r, r] = 1
    back[1, block - r[1:], half + r[1:]] = 1
    back[1, 0, 2 * half] = 1
    back = jnp.asarray(back.astype(ml_dtypes.bfloat16))

    piece = (3, 2, hb, width)
    dma = pltpu.SemaphoreType.DMA
    vmem = lambda *shape: pltpu.VMEM(shape, jnp.bfloat16)
    wide = lambda *shape: pltpu.VMEM(shape, jnp.float32)
    return pl.pallas_call(
        functools.partial(step_kernel, dims),
        out_shape=jax.ShapeDtypeStruct(spectral_state.shape, jnp.float32),
        in_specs=[VMEM] * 10 + [pl.BlockSpec(memory_space=pl.ANY)],
        out_specs=VMEM,
        scratch_shapes=[
            vmem(2, chunks, *piece), vmem(3, 2, EDGE, width),
            vmem(chunks, 2, 2, chips, *piece), vmem(2, chips, 3, 2, EDGE, width),
            vmem(6 * hb, length), vmem(6 * hb, length),
            vmem(chunks, slots, 2 * hb, 3 * block), vmem(chunks, slots, 2 * hb, 3 * block),
            vmem(3 * block, length // chunks), wide(3 * block, length), vmem(5 * block, length),
            vmem(length, length), vmem(length, length), vmem(length, length),
            wide(chunks, 2, hb, length), wide(chunks, 2, hb, length),
            wide(block, width), wide(block, width),
            vmem(chunks, slots, 2 * hb, 5 * block), vmem(chunks, slots, 2 * hb, 5 * block),
            vmem(10 * hb, length),
            vmem(chunks, 2, chips, 2, *piece), vmem(chunks, chips, 2, *piece),
            wide(2, *piece), vmem(chunks, chips, 2, *piece), vmem(chunks, chips, 2, *piece),
            vmem(chunks, *piece), vmem(chunks, *piece), vmem(chunks, *piece),
            vmem(3, 2, EDGE, width),
            dma((chunks,)), dma((chunks,)),
            dma((2, chips)), dma((2, chips)),
            dma((chunks, 2, chips)), dma((chunks, 2, chips)),
            dma((chunks, 2, chips)), dma((chunks, 2, chips)),
            dma((chunks, slots)), dma((chunks, slots)), dma((chunks,)),
            dma((chunks, slots)), dma((chunks, slots)), dma((chunks,)),
            dma((chunks,)), dma((chunks,)),
            dma((chunks, chips)), dma((chunks, chips)),
            dma((chunks,)), dma((chunks,)),
            dma(()), dma(()), dma(()),
        ],
        compiler_params=pltpu.CompilerParams(
            collective_id=0, has_side_effects=True, vmem_limit_bytes=56 * 2**20
        ),
        name="averaged_step",
    )(spectral_state, into, back, info, ky, own_kx, phase.reshape(1, 1),
      *angle_tables(length, width, owners), packed)


def cube_table(length, slots, chunks):
    half = length // (2 * slots)
    rows = half * np.arange(slots)[:, None] + np.arange(half)
    cosine, sine = circle(rows[:, :, None] * np.arange(length), length)
    packed = np.stack([cosine, -sine], axis=1)
    packed[0, 1, 0] = circle(length // 2 * np.arange(length), length)[0]
    packed = packed.reshape(slots, 2, chunks, half // chunks, length).transpose(2, 0, 1, 3, 4)
    return packed.reshape(length, length).astype(ml_dtypes.bfloat16)


def signal_all(barrier, peers):
    for space, avg in peers:
        pl.semaphore_signal(
            barrier, inc=1, device_id={"space": space, "avg": avg}, device_id_type=MESH
        )


def only_row(n, value, rows):
    spot = lax.broadcasted_iota(jnp.int32, (rows, value.shape[-1]), 0)
    return jnp.where(spot == n, jnp.broadcast_to(value, (rows, value.shape[-1])), 0.0)


def cube_kernel(
    dims, state, order_rows, info, ky, own_kx, phase, blocks, steps, fines, packed_hbm, result,
    ph_mine, ph_got, moved, top, gx, eg, rows_c, rows_s, half, arr, arr_t, grid, products, packed,
    ct, st, sine, cosine, end_sine, end_cosine, fh, ret, lhs, stage, rsin, xs, rb, lt, le,
    ph_s, ph_r, x_s, x_r, c_s, c_r, g_s, eg_s, eg_r, a_s, a_r, l_s,
    b_s, b_r, m_s, d_s, d_r, y_s, y_r, k_s, le_s, le_r, bring_s,
):
    slots, chunks, hb, width, block = dims
    length, reach = slots * block, block // 2
    g, a, q, core = positions()
    side = g // (slots // 2)
    pair_block = g + side * (slots - 1 - 2 * g)
    me = 2 * pair_block + q
    mirror = slots - 1 - g
    partner = 2 * q + 1 - core
    low, high = side == 0, side == 1
    bring = pltpu.make_async_copy(packed_hbm, packed, bring_s)

    def place(slot):
        b = slot // 2
        return b + side * (slots - 1 - 2 * b), 2 * (slot % 2) + core

    def chip(m):
        return (q + m) % 2

    top_tile = jnp.zeros((EDGE, width), jnp.float32)
    for f in range(3):
        for i in range(2):
            plane = state[f, i].astype(jnp.bfloat16)
            top_tile = top_tile + only_row(2 * f + i, state[f, i, 0:1, :], EDGE)
            picked = jnp.dot(order_rows[side], plane, preferred_element_type=jnp.float32)
            picked = picked.astype(jnp.bfloat16)
            for h in range(2):
                for t in range(chunks):
                    spot = h * reach + t * hb
                    moved[h, t, f, i] = picked[spot : spot + hb]
    top[...] = top_tile.astype(jnp.bfloat16)
    ph_mine[...] = jnp.broadcast_to(phase[...], ph_mine.shape)

    barrier = pltpu.get_barrier_semaphore()
    near = [place((me + d) % slots) for d in range(1, slots)] + [(g, partner)]
    near += [(mirror, 2 * chip(m) + core) for m in range(2)]
    across = edge_partner(g, slots)
    below = [(across, c) for c in range(2)] + [(slots - 1 - across, c) for c in range(2)]
    source = edge_partner(pair_block, slots)
    above = [(source, c) for c in range(4)]
    signal_all(barrier, near)

    @pl.when(high)
    def _():
        signal_all(barrier, below)

    @pl.when(q == 0)
    def _():
        signal_all(barrier, above)
    pl.semaphore_wait(barrier, len(near) + len(below) * side + len(above) * (1 - q))

    def build_factors():
        turn = chosen_phase()[:, 0:1]
        for t in range(chunks):
            for s in range(2):
                def one(j, carry, t=t, s=s):
                    span = pl.ds(pl.multiple_of(j * 256, 256), 256)
                    factors = wave_factors(column(info, t, s), ky[:, span], turn)
                    sine[t, s, :, span], cosine[t, s, :, span] = factors
                    return carry
                lax.fori_loop(0, length // 256, one, 0)

    def chosen_phase():
        keep = 1.0 - jnp.abs(q - side).astype(jnp.float32)
        return ph_got[0:1] + keep * (ph_mine[0:1] - ph_got[0:1])

    def build_tables():
        for c in range(2):
            for m in range(2):
                owner = 2 * chip(m) + (core + c) % 2
                first = (blocks[0, pl.ds(owner, 1), :], blocks[1, pl.ds(owner, 1), :])

                def one(h, carry, j=c * 2 + m, first=first):
                    begin = turned(first, (steps[0, pl.ds(h, 1), :], steps[1, pl.ds(h, 1), :]))
                    cos_rows, sin_rows = turned(begin, (fines[0], fines[1]))
                    at = pl.ds(pl.multiple_of(j * width + h * FINE, FINE), FINE)
                    ct[at, :] = cos_rows.astype(jnp.bfloat16)
                    st[at, :] = sin_rows.astype(jnp.bfloat16)
                    return carry
                lax.fori_loop(0, width // FINE, one, 0)

    swap_phase = remote(ph_mine, ph_got, ph_s, ph_r, g, 2 * chip(1) + core)

    def bring_own(t):
        return remote(moved.at[chip(1), t], gx.at[t, side, 0, 1], x_s.at[t, 0], x_r.at[t, 0],
                      g, 2 * chip(1) + core)

    def bring_mirror(t, m):
        return remote(moved.at[chip(m), t], gx.at[t, side, 0, m], x_s.at[t, 1 + m], x_r.at[t, 1 + m],
                      mirror, 2 * chip(m) + core)

    def keep_own(t):
        return pltpu.make_async_copy(moved.at[q, t], gx.at[t, side, 0, 0], g_s.at[t])

    def over_cores(t, kind, m):
        role = (1 - side) if kind else side
        piece = gx.at[t, role, 0, m] if kind + m else moved.at[q, t]
        return remote(piece, gx.at[t, role, 1, m], c_s.at[t, kind, m], c_r.at[t, kind, m], g, partner)

    edges = [
        remote(top, eg.at[c, q], eg_s.at[k, c], eg_r.at[c, q], space, (core + c) % 2)
        for k, space in enumerate((across, slots - 1 - across)) for c in range(2)
    ]

    def to_grid(t, d):
        to = (me + d) % slots
        space, avg = place(to)
        return remote(half.at[t, to], arr.at[t, me], a_s.at[t, d], a_r.at[t, d], space, avg)

    def to_rows(t, d):
        to = (me + d) % slots
        space, avg = place(to)
        return remote(fh.at[t, to], ret.at[t, me], b_s.at[t, d], b_r.at[t, d], space, avg)

    def sum_cores(t):
        return remote(stage.at[t, 1], rsin.at[t], d_s.at[t], d_r.at[t], g, partner)

    def give_own(t):
        return remote(xs.at[t, 1, side], rb.at[t, 0, q], y_s.at[t, 0], y_r.at[t, 0],
                      g, 2 * chip(1) + core)

    def give_mirror(t, m):
        return remote(xs.at[t, m, 1 - side], rb.at[t, 1, q], y_s.at[t, 1 + m], y_r.at[t, 1 + m],
                      mirror, 2 * chip(m) + core)

    def give_self(t):
        return pltpu.make_async_copy(xs.at[t, 0, side], rb.at[t, 0, q], k_s.at[t])

    last = [
        remote(lt.at[m], le.at[side], le_s.at[m], le_r.at[side], source, 2 * chip(m) + core)
        for m in range(2)
    ]

    swap_phase.start()

    @pl.when(high)
    def _():
        for copy in edges:
            copy.start()
    for t in range(chunks):
        for m in range(2):
            bring_mirror(t, m).start()
        bring_own(t).start()
        over_cores(t, 0, 0).start()
        keep_own(t).start()
    bring.start()

    @pl.when(q != 0)
    def _():
        eg[...] = jnp.zeros_like(eg)

    @pl.when(low)
    def _():
        le[...] = jnp.zeros_like(le)
    build_tables()
    swap_phase.wait_recv()
    build_factors()
    scale = chosen_phase()[:, 1:2] * (1.0 / length)

    @pl.when(q == 0)
    def _():
        for c in range(2):
            for m in range(2):
                remote(top, eg.at[c, m], eg_s.at[0, c], eg_r.at[c, m], g, partner).wait_recv()

    def rotate(t):
        bring_own(t).wait_recv()
        over_cores(t, 0, 1).start()
        for m in range(2):
            bring_mirror(t, m).wait_recv()
            over_cores(t, 1, m).start()
        keep_own(t).wait()
        for kind in range(2):
            for m in range(2):
                over_cores(t, kind, m).wait_recv()
        own_pair = column(info, t, 2) > 0.5
        for j in range(4):
            c, m = divmod(j, 2)
            span = slice(j * width, (j + 1) * width)
            turned_rows = []
            for s in range(2):
                piece = gx.at[t, s, c, m]
                fields = [[piece[f, i].astype(jnp.float32) for i in range(2)] for f in range(3)]
                if s == 1 and t == 0:
                    put = column(info, t, 3) > 0.5
                    tile = eg[c, m].astype(jnp.float32)
                    for f in range(3):
                        for i in range(2):
                            n = 2 * f + i
                            row = jnp.broadcast_to(tile[n : n + 1], (hb, width))
                            fields[f][i] = jnp.where(put, row, fields[f][i])
                turned_rows.append(wave_exponential(
                    fields, column(info, t, s), ky[:, span], (sine[t, s, :, span], cosine[t, s, :, span])
                ))
            for f in range(3):
                (re0, im0), (re1, im1) = turned_rows[0][f], turned_rows[1][f]
                for i, value in enumerate((
                    jnp.where(own_pair, re0, re0 + re1), jnp.where(own_pair, re1, im0 - im1)
                )):
                    rows_c[(i * 3 + f) * hb : (i * 3 + f + 1) * hb, span] = value.astype(jnp.bfloat16)
                for i, value in enumerate((
                    jnp.where(own_pair, -im0, -(im0 + im1)), jnp.where(own_pair, -im1, re0 - re1)
                )):
                    rows_s[(i * 3 + f) * hb : (i * 3 + f + 1) * hb, span] = value.astype(jnp.bfloat16)
        tile = min(length, max(block, 256))
        for y in range(0, length, tile):
            value = (
                jnp.dot(rows_c[...], ct[:, y : y + tile], preferred_element_type=jnp.float32)
                + jnp.dot(rows_s[...], st[:, y : y + tile], preferred_element_type=jnp.float32)
            ).astype(jnp.bfloat16)
            for b in range(tile // block):
                for i in range(2):
                    for f in range(3):
                        half[t, y // block + b, i * hb : (i + 1) * hb, f * block : (f + 1) * block] = (
                            value[(i * 3 + f) * hb : (i * 3 + f + 1) * hb, b * block : (b + 1) * block]
                        )
        for d in sending(slots):
            to_grid(t, d).start()
        pltpu.make_async_copy(half.at[t, me], arr.at[t, me], l_s.at[t]).start()

    depth = length // chunks

    def on_grid(t):
        for d in range(1, slots):
            to_grid(t, d).wait_recv()
        pltpu.make_async_copy(half.at[t, me], arr.at[t, me], l_s.at[t]).wait()
        together = max(1, 128 // (2 * hb))
        for p in range(0, slots, together):
            value = arr[t, p : p + together].astype(jnp.float32)
            value = value.reshape(together * 2 * hb, 3 * block)
            spot = p * 2 * hb
            arr_t[:, spot : spot + together * 2 * hb] = value.T.astype(jnp.bfloat16)
        for x in range(0, length, 256):
            value = jnp.dot(
                arr_t[...], packed[t * depth : (t + 1) * depth, x : x + 256],
                preferred_element_type=jnp.float32,
            )
            if t:
                value = value + grid[:, x : x + 256]
            if t < chunks - 1:
                grid[:, x : x + 256] = value
            else:
                value = value * (1.0 / length)
                east, north, height = (value[i * block : (i + 1) * block] for i in range(3))
                for k, pair in enumerate((
                    east * east, east * north, north * north, east * height, north * height
                )):
                    products[k * block : (k + 1) * block, x : x + 256] = pair.astype(jnp.bfloat16)

    bring.wait()
    for t in range(chunks):
        rotate(t)
        if t:
            on_grid(t - 1)
    end_sine[...], end_cosine[...] = wave_factors(own_kx[...], ky[:, :width], time_step)
    on_grid(chunks - 1)

    for t in range(chunks):
        for k in range(0, depth, 256):
            value = lax.dot_general(
                packed[t * depth + k : t * depth + k + 256, :], products[...], DIMS_NT,
                preferred_element_type=jnp.float32,
            ).astype(jnp.bfloat16)
            for n in range(256 // (2 * hb)):
                fh[t, k // (2 * hb) + n] = value[n * 2 * hb : (n + 1) * 2 * hb]
        for d in sending(slots):
            to_rows(t, d).start()
        pltpu.make_async_copy(fh.at[t, me], ret.at[t, me], m_s.at[t]).start()

    def pass_on(t):
        sum_cores(t).wait_recv()
        for m in range(2):
            for s in range(2):
                value = stage[t, 0, m, s].astype(jnp.float32) + rsin[t, m, s].astype(jnp.float32)
                xs[t, m, s] = value.astype(jnp.bfloat16)
                if t == 0 and s == 1:
                    tile = jnp.zeros((EDGE, width), jnp.float32)
                    for f in range(3):
                        for i in range(2):
                            tile = tile + only_row(2 * f + i, value[f, i, 0:1], EDGE)
                    lt[m] = tile.astype(jnp.bfloat16)
        for m in range(2):
            give_mirror(t, m).start()
        give_own(t).start()
        give_self(t).start()
        if t == 0:
            @pl.when(q == 0)
            def _():
                for copy in last:
                    copy.start()

    for t in range(chunks):
        for d in range(1, slots):
            to_rows(t, d).wait_recv()
        pltpu.make_async_copy(fh.at[t, me], ret.at[t, me], m_s.at[t]).wait()
        for p in range(slots):
            for k in range(5):
                lhs[k * 2 * hb : (k + 1) * 2 * hb, p * block : (p + 1) * block] = (
                    ret[t, p, :, k * block : (k + 1) * block]
                )
        own_pair = column(info, t, 2) > 0.5
        for j in range(4):
            c, m = divmod(j, 2)
            span = slice(j * width, (j + 1) * width)
            by_c = lax.dot_general(lhs[...], ct[span, :], DIMS_NT, preferred_element_type=jnp.float32)
            by_s = lax.dot_general(lhs[...], st[span, :], DIMS_NT, preferred_element_type=jnp.float32)

            def part(values, k, i):
                return values[(2 * k + i) * hb : (2 * k + i + 1) * hb] * scale

            for s in range(2):
                real, imag = [], []
                for k in range(5):
                    rc, ic = part(by_c, k, 0), part(by_c, k, 1)
                    rs, iz = part(by_s, k, 0), part(by_s, k, 1)
                    real.append(jnp.where(own_pair, (ic if s else rc), (rc - iz if s else rc + iz)))
                    imag.append(jnp.where(own_pair, -(iz if s else rs), (-ic if s else ic) - rs))
                kx, kyj = column(info, t, s), ky[:, span]
                tendency = [
                    (kx * imag[u] + kyj * imag[v], -(kx * real[u] + kyj * real[v]))
                    for u, v in ((0, 1), (1, 2), (3, 4))
                ]
                back = wave_exponential(
                    tendency, kx, kyj, (-sine[t, s, :, span], cosine[t, s, :, span])
                )
                for f in range(3):
                    for i in range(2):
                        stage[t, c, m, s, f, i] = back[f][i].astype(jnp.bfloat16)
        sum_cores(t).start()
        pass_on(t)

    for t in range(chunks):
        bring_own(t).wait_send()
        for m in range(2):
            bring_mirror(t, m).wait_send()
        for kind in range(2):
            for m in range(2):
                over_cores(t, kind, m).wait_send()
        for d in range(1, slots):
            to_grid(t, d).wait_send()
            to_rows(t, d).wait_send()
        sum_cores(t).wait_send()
    swap_phase.wait_send()

    @pl.when(high)
    def _():
        for copy in edges:
            copy.wait_send()
        for k in range(2):
            remote(lt.at[0], le.at[k], le_s.at[0], le_r.at[k], g, partner).wait_recv()

    for t in range(chunks):
        give_own(t).wait_recv()
        for m in range(2):
            give_mirror(t, m).wait_recv()
        give_self(t).wait()

    edge = le[0].astype(jnp.float32) + le[1].astype(jnp.float32)
    for f in range(3):
        for i in range(2):
            pieces = [
                rb[t, 0, h, f, i].astype(jnp.float32) + rb[t, 1, h, f, i].astype(jnp.float32)
                for h in range(2) for t in range(chunks)
            ]
            n = 2 * f + i
            pieces[0] = jnp.where(
                column(info, 0, 4) > 0.5, jnp.broadcast_to(edge[n : n + 1], (hb, width)), pieces[0]
            )
            rows = jnp.concatenate(pieces, axis=0).astype(jnp.bfloat16)
            averaged = jnp.dot(order_rows[side], rows, preferred_element_type=jnp.float32)
            result[f, i] = state[f, i] + time_step * averaged
    fields = [[result[f, i] for i in range(2)] for f in range(3)]
    advanced = wave_exponential(fields, own_kx[...], ky[:, :width], (end_sine[...], end_cosine[...]))
    for f in range(3):
        for i in range(2):
            result[f, i] = advanced[f][i]

    for t in range(chunks):
        give_own(t).wait_send()
        for m in range(2):
            give_mirror(t, m).wait_send()

    @pl.when(q == 0)
    def _():
        for copy in last:
            copy.wait_send()


def cube_step(spectral_state, phase_index, weight_count):
    slots, owners = lax.axis_size("space"), lax.axis_size("avg")
    block, width = spectral_state.shape[2:]
    length, half = block * slots, block // 2
    chunks = max(1, half // CHUNK_ROWS)
    hb = half // chunks
    dims = (slots, chunks, hb, width, block)
    g, a = lax.axis_index("space"), lax.axis_index("avg")
    q, core = a // 2, a % 2
    low = g < slots // 2
    phase = phase_index[0].astype(jnp.float32) * phase_step
    weight = weight_count[0].astype(jnp.float32) / (weight_scale * owners)
    phase = jnp.where(jnp.arange(128) == 0, phase, weight).reshape(1, 128)

    m, c = jnp.arange(2, dtype=jnp.int32), jnp.arange(2, dtype=jnp.int32)[:, None]
    order = (2 * ((q + m) % 2) + (core + c) % 2).reshape(-1)
    columns = (order[:, None] * width + jnp.arange(width, dtype=jnp.int32)).reshape(1, -1)
    ky = wave_of(columns, length)
    packed = jnp.asarray(cube_table(length, slots, chunks))

    base = block * jnp.where(low, g, slots - 1 - g) + half * q
    direct = base + jnp.arange(half, dtype=jnp.int32)
    mirrored = jnp.where(direct == 0, length // 2, length - direct)
    begins = jnp.arange(half) == 0
    zeros = jnp.zeros((half,), jnp.float32)
    info = jnp.stack([
        wave_of(direct, length), wave_of(mirrored, length), (direct == 0).astype(jnp.float32),
        (begins & (q == 0)).astype(jnp.float32), (begins & ~low).astype(jnp.float32),
        zeros, zeros, zeros,
    ], axis=1).reshape(chunks, hb, 8)
    own_kx = wave_of(g * block + jnp.arange(block, dtype=jnp.int32)[:, None], length)

    r = np.arange(block)
    rows = np.zeros((2, block, block), np.float32)
    rows[0, r, r] = 1
    rows[1, r, -r % block] = 1
    rows = jnp.asarray(rows.astype(ml_dtypes.bfloat16))

    piece = (3, 2, hb, width)
    dma = pltpu.SemaphoreType.DMA
    vmem = lambda *shape: pltpu.VMEM(shape, jnp.bfloat16)
    wide = lambda *shape: pltpu.VMEM(shape, jnp.float32)
    return pl.pallas_call(
        functools.partial(cube_kernel, dims),
        out_shape=jax.ShapeDtypeStruct(spectral_state.shape, jnp.float32),
        in_specs=[VMEM] * 9 + [pl.BlockSpec(memory_space=pl.ANY)],
        out_specs=VMEM,
        scratch_shapes=[
            wide(8, 128), wide(8, 128),
            vmem(2, chunks, *piece), vmem(EDGE, width),
            vmem(chunks, 2, 2, 2, *piece), vmem(2, 2, EDGE, width),
            vmem(6 * hb, length), vmem(6 * hb, length),
            vmem(chunks, slots, 2 * hb, 3 * block), vmem(chunks, slots, 2 * hb, 3 * block),
            vmem(3 * block, length // chunks), wide(3 * block, length), vmem(5 * block, length),
            vmem(length, length), vmem(length, length), vmem(length, length),
            wide(chunks, 2, hb, length), wide(chunks, 2, hb, length),
            wide(block, width), wide(block, width),
            vmem(chunks, slots, 2 * hb, 5 * block), vmem(chunks, slots, 2 * hb, 5 * block),
            vmem(10 * hb, length),
            vmem(chunks, 2, 2, 2, *piece), vmem(chunks, 2, 2, *piece),
            vmem(chunks, 2, 2, *piece), vmem(chunks, 2, 2, *piece),
            vmem(2, EDGE, width), vmem(2, EDGE, width),
            dma(()), dma(()),
            dma((chunks, 3)), dma((chunks, 3)),
            dma((chunks, 2, 2)), dma((chunks, 2, 2)), dma((chunks,)),
            dma((2, 2)), dma((2, 2)),
            dma((chunks, slots)), dma((chunks, slots)), dma((chunks,)),
            dma((chunks, slots)), dma((chunks, slots)), dma((chunks,)),
            dma((chunks,)), dma((chunks,)),
            dma((chunks, 3)), dma((chunks, 3)), dma((chunks,)),
            dma((2,)), dma((2,)), dma(()),
        ],
        compiler_params=pltpu.CompilerParams(
            collective_id=0, has_side_effects=True, vmem_limit_bytes=56 * 2**20
        ),
        name="averaged_step",
    )(spectral_state, rows, info, ky, own_kx, phase,
      *angle_tables(length, width, owners), packed)


CHUNK_ROWS = 16


def solution(mesh):
    in_specs = (P(None, None, "space", "avg"), P("avg"), P("avg"))
    out_specs = P(None, None, "space", "avg")
    body = cube_step if mesh.shape["avg"] == 4 else per_device
    return jax.shard_map(
        body, mesh=mesh, in_specs=in_specs, out_specs=out_specs, check_vma=False
    )
```

profile of v0, /device:TPU:17, one launch (start us, length us, event | category | flops | bytes accessed | tf_op | source)
XLA Modules:
  0.0 80.2 jit_solution(13119273077610092959)
XLA Ops:
  1.3 0.5 compare_select_fusion.6.phase
  1.8 0.1 add_multiply_fusion
  1.9 0.1 mul.69
  2.0 0.1 add_bitcast_fusion
  2.1 0.6 fusion.18.ky
  2.7 0.7 fusion.3.own_kx
  3.5 0.7 stack.5.info
  4.2 73.9 %averaged_step.1 = f32[3,2,128,256]{3,2,1,0:T(8,128)} custom-call(f32[3,2,128,256]{3,2,1,0:T(8,128)} %state.1, bf16[2,128,128]{2,1,0:T(8,128)(2,1)} %constant.139.clone.order_rows, f32[4,16,8]{2,1,0:T(8,128)} %stack.5.info, f32[1,1024]{1,0:T(1,128)} %fusion.18.ky, f32[128,1]{1,0:T(8,128)} %fusion.3.own_kx, f32[1,128]{1,0:T(1,128)} %compare_select_fusion.6.phase, ...), custom_call_target="tpu_custom_call" | custom-call | tf_op jit(solution)/shard_map/averaged_step/pallas_call | solution.py:1033
  78.1 2.1 %copy.16 = f32[3,2,128,256]{3,2,1,0:T(8,128)} copy(f32[3,2,128,256]{3,2,1,0:T(8,128)} %averaged_step.1) | data formatting | bytes 1572864
  (7 shorter events, 0.1 us)
where the time goes:
time: 81 us; the launch traced here: 80.2 us
  Pallas kernels  73.9 us (91%)
  local copies, waits for them, and re-layouts  2.93 us (4%)
  other arithmetic  2.03 us (3%)
  between operations  1.34 us (2%)
    pallas_call x1, Pallas kernels, cube_step(): pl.pallas_call(functools.partial(cube_kernel, dims), out_shape=jax.ShapeD...  73.9 us
    unnamed x2, local copies, waits for them, and re-layouts  2.11 us

commit v1 on v0

--- a/solution.py
+++ b/solution.py
@@ -572,16 +572,6 @@
       *angle_tables(length, width, owners), packed)
 
 
-def cube_table(length, slots, chunks):
-    half = length // (2 * slots)
-    rows = half * np.arange(slots)[:, None] + np.arange(half)
-    cosine, sine = circle(rows[:, :, None] * np.arange(length), length)
-    packed = np.stack([cosine, -sine], axis=1)
-    packed[0, 1, 0] = circle(length // 2 * np.arange(length), length)[0]
-    packed = packed.reshape(slots, 2, chunks, half // chunks, length).transpose(2, 0, 1, 3, 4)
-    return packed.reshape(length, length).astype(ml_dtypes.bfloat16)
-
-
 def signal_all(barrier, peers):
     for space, avg in peers:
         pl.semaphore_signal(
@@ -595,11 +585,11 @@
 
 
 def cube_kernel(
-    dims, state, order_rows, info, ky, own_kx, phase, blocks, steps, fines, packed_hbm, result,
-    ph_mine, ph_got, moved, top, gx, eg, rows_c, rows_s, half, arr, arr_t, grid, products, packed,
+    dims, phase_ref, weight_ref, state_hbm, table_hbm, result,
+    state, order_rows, info, ky, own_kx, parts, ph_mine, ph_got, moved, top, gx, eg, rows_c, rows_s, half, arr, arr_t, grid, products, packed,
     ct, st, sine, cosine, end_sine, end_cosine, fh, ret, lhs, stage, rsin, xs, rb, lt, le,
     ph_s, ph_r, x_s, x_r, c_s, c_r, g_s, eg_s, eg_r, a_s, a_r, l_s,
-    b_s, b_r, m_s, d_s, d_r, y_s, y_r, k_s, le_s, le_r, bring_s,
+    b_s, b_r, m_s, d_s, d_r, y_s, y_r, k_s, le_s, le_r, load_s,
 ):
     slots, chunks, hb, width, block = dims
     length, reach = slots * block, block // 2
@@ -610,7 +600,6 @@
     mirror = slots - 1 - g
     partner = 2 * q + 1 - core
     low, high = side == 0, side == 1
-    bring = pltpu.make_async_copy(packed_hbm, packed, bring_s)
 
     def place(slot):
         b = slot // 2
@@ -618,20 +607,6 @@
 
     def chip(m):
         return (q + m) % 2
-
-    top_tile = jnp.zeros((EDGE, width), jnp.float32)
-    for f in range(3):
-        for i in range(2):
-            plane = state[f, i].astype(jnp.bfloat16)
-            top_tile = top_tile + only_row(2 * f + i, state[f, i, 0:1, :], EDGE)
-            picked = jnp.dot(order_rows[side], plane, preferred_element_type=jnp.float32)
-            picked = picked.astype(jnp.bfloat16)
-            for h in range(2):
-                for t in range(chunks):
-                    spot = h * reach + t * hb
-                    moved[h, t, f, i] = picked[spot : spot + hb]
-    top[...] = top_tile.astype(jnp.bfloat16)
-    ph_mine[...] = jnp.broadcast_to(phase[...], ph_mine.shape)
 
     barrier = pltpu.get_barrier_semaphore()
     near = [place((me + d) % slots) for d in range(1, slots)] + [(g, partner)]
@@ -649,11 +624,65 @@
     @pl.when(q == 0)
     def _():
         signal_all(barrier, above)
+    loads = [
+        pltpu.make_async_copy(source_ref, target, load_s.at[n])
+        for n, (source_ref, target) in enumerate((
+            (state_hbm, state), (table_hbm, parts)
+        ))
+    ]
+    for copy in loads:
+        copy.start()
+
+    def wave(spot):
+        return jnp.where(spot >= length // 2, spot - length, spot).astype(jnp.float32) * (2.0 / length)
+
+    lane = lax.broadcasted_iota(jnp.int32, (hb, 128), 1)
+    for t in range(chunks):
+        spot = lax.broadcasted_iota(jnp.int32, (hb, 128), 0) + t * hb
+        direct = spot + (block * pair_block + reach * q)
+        mirrored = jnp.where(direct == 0, length // 2, length - direct)
+        begins = jnp.where(spot == 0, 1.0, 0.0)
+        info[t] = jnp.where(lane == 0, wave(direct), jnp.where(lane == 1, wave(mirrored), jnp.where(
+            lane == 2, jnp.where(direct == 0, 1.0, 0.0), jnp.where(
+                lane == 3, begins * (1 - q).astype(jnp.float32), begins * side.astype(jnp.float32)
+            )
+        )))
+    own_kx[...] = wave(lax.broadcasted_iota(jnp.int32, (block, 128), 0) + g * block)
+    for j in range(4):
+        c, m = divmod(j, 2)
+        owner = 2 * ((q + m) % 2) + (core + c) % 2
+        spot = lax.broadcasted_iota(jnp.int32, (1, width), 1) + owner * width
+        ky[:, j * width : (j + 1) * width] = wave(spot)
+    down = lax.broadcasted_iota(jnp.int32, (block, block), 0)
+    along = lax.broadcasted_iota(jnp.int32, (block, block), 1)
+    turned_down = jnp.where(down == 0, 0, block - down)
+    order_rows[...] = jnp.where(
+        along == down + side * (turned_down - down), 1.0, 0.0
+    ).astype(jnp.bfloat16)
+    lane = lax.broadcasted_iota(jnp.int32, ph_mine.shape, 1)
+    ph_mine[...] = jnp.where(
+        lane == 0, phase_ref[0].astype(jnp.float32) * phase_step,
+        weight_ref[0].astype(jnp.float32) / (weight_scale * 4),
+    )
+    loads[0].wait()
+
+    top_tile = jnp.zeros((EDGE, width), jnp.float32)
+    for f in range(3):
+        for i in range(2):
+            plane = state[f, i].astype(jnp.bfloat16)
+            top_tile = top_tile + only_row(2 * f + i, state[f, i, 0:1, :], EDGE)
+            picked = jnp.dot(order_rows[...], plane, preferred_element_type=jnp.float32)
+            picked = picked.astype(jnp.bfloat16)
+            for h in range(2):
+                for t in range(chunks):
+                    spot = h * reach + t * hb
+                    moved[h, t, f, i] = picked[spot : spot + hb]
+    top[...] = top_tile.astype(jnp.bfloat16)
     pl.semaphore_wait(barrier, len(near) + len(below) * side + len(above) * (1 - q))
 
-    def build_factors():
+    def build_factors(t):
         turn = chosen_phase()[:, 0:1]
-        for t in range(chunks):
+        if True:
             for s in range(2):
                 def one(j, carry, t=t, s=s):
                     span = pl.ds(pl.multiple_of(j * 256, 256), 256)
@@ -666,15 +695,41 @@
         keep = 1.0 - jnp.abs(q - side).astype(jnp.float32)
         return ph_got[0:1] + keep * (ph_mine[0:1] - ph_got[0:1])
 
+    steps, owners = width // FINE, 4
+
+    def begin_rows(owner, h):
+        return turned(
+            (parts[pl.ds(2 * (FINE + steps) + owner, 1)], parts[pl.ds(2 * (FINE + steps) + owners + owner, 1)]),
+            (parts[pl.ds(2 * FINE + h, 1)], parts[pl.ds(2 * FINE + steps + h, 1)]),
+        )
+
+    def fine_rows(begin):
+        return turned(begin, (parts[0:FINE], parts[FINE : 2 * FINE]))
+
+    def build_packed():
+        def one(n, carry):
+            begin = begin_rows(n // steps, n % steps)
+            cos_rows, sin_rows = fine_rows(begin)
+            slot, t = n // chunks, n % chunks
+            at = pl.multiple_of((t * slots + slot) * 2 * hb, 2 * hb)
+            packed[pl.ds(at, hb), :] = cos_rows.astype(jnp.bfloat16)
+            packed[pl.ds(at + hb, hb), :] = (-sin_rows).astype(jnp.bfloat16)
+            return carry
+        lax.fori_loop(0, length // (2 * FINE), one, 0)
+        down = lax.broadcasted_iota(jnp.int32, (hb, length), 0)
+        along = lax.broadcasted_iota(jnp.int32, (hb, length), 1)
+        rest = packed[hb : 2 * hb, :].astype(jnp.float32)
+        packed[hb : 2 * hb, :] = jnp.where(
+            down == 0, 1.0 - 2.0 * (along % 2).astype(jnp.float32), rest
+        ).astype(jnp.bfloat16)
+
     def build_tables():
         for c in range(2):
             for m in range(2):
                 owner = 2 * chip(m) + (core + c) % 2
-                first = (blocks[0, pl.ds(owner, 1), :], blocks[1, pl.ds(owner, 1), :])
-
-                def one(h, carry, j=c * 2 + m, first=first):
-                    begin = turned(first, (steps[0, pl.ds(h, 1), :], steps[1, pl.ds(h, 1), :]))
-                    cos_rows, sin_rows = turned(begin, (fines[0], fines[1]))
+
+                def one(h, carry, j=c * 2 + m, owner=owner):
+                    cos_rows, sin_rows = fine_rows(begin_rows(owner, h))
                     at = pl.ds(pl.multiple_of(j * width + h * FINE, FINE), FINE)
                     ct[at, :] = cos_rows.astype(jnp.bfloat16)
                     st[at, :] = sin_rows.astype(jnp.bfloat16)
@@ -739,14 +794,15 @@
     def _():
         for copy in edges:
             copy.start()
-    for t in range(chunks):
+    def launch(t):
         for m in range(2):
             bring_mirror(t, m).start()
         bring_own(t).start()
         over_cores(t, 0, 0).start()
         keep_own(t).start()
-    bring.start()
-
+
+    launch(0)
+    pass
     @pl.when(q != 0)
     def _():
         eg[...] = jnp.zeros_like(eg)
@@ -754,16 +810,15 @@
     @pl.when(low)
     def _():
         le[...] = jnp.zeros_like(le)
-    build_tables()
     swap_phase.wait_recv()
-    build_factors()
     scale = chosen_phase()[:, 1:2] * (1.0 / length)
 
-    @pl.when(q == 0)
-    def _():
-        for c in range(2):
-            for m in range(2):
-                remote(top, eg.at[c, m], eg_s.at[0, c], eg_r.at[c, m], g, partner).wait_recv()
+    def meet_edges():
+        @pl.when(q == 0)
+        def _():
+            for c in range(2):
+                for m in range(2):
+                    remote(top, eg.at[c, m], eg_s.at[0, c], eg_r.at[c, m], g, partner).wait_recv()
 
     def rotate(t):
         bring_own(t).wait_recv()
@@ -849,12 +904,25 @@
                 )):
                     products[k * block : (k + 1) * block, x : x + 256] = pair.astype(jnp.bfloat16)
 
-    bring.wait()
-    for t in range(chunks):
-        rotate(t)
-        if t:
-            on_grid(t - 1)
-    end_sine[...], end_cosine[...] = wave_factors(own_kx[...], ky[:, :width], time_step)
+    loads[1].wait()
+    build_tables()
+    build_factors(0)
+    launch(1)
+    build_factors(1)
+    meet_edges()
+    rotate(0)
+    launch(2)
+    build_packed()
+    build_factors(2)
+    rotate(1)
+    launch(3)
+    on_grid(0)
+    build_factors(3)
+    rotate(2)
+    on_grid(1)
+    rotate(3)
+    on_grid(2)
+    end_sine[...], end_cosine[...] = wave_factors(own_kx[:, 0:1], ky[:, :width], time_step)
     on_grid(chunks - 1)
 
     for t in range(chunks):
@@ -969,13 +1037,13 @@
                 column(info, 0, 4) > 0.5, jnp.broadcast_to(edge[n : n + 1], (hb, width)), pieces[0]
             )
             rows = jnp.concatenate(pieces, axis=0).astype(jnp.bfloat16)
-            averaged = jnp.dot(order_rows[side], rows, preferred_element_type=jnp.float32)
+            averaged = jnp.dot(order_rows[...], rows, preferred_element_type=jnp.float32)
             result[f, i] = state[f, i] + time_step * averaged
     fields = [[result[f, i] for i in range(2)] for f in range(3)]
-    advanced = wave_exponential(fields, own_kx[...], ky[:, :width], (end_sine[...], end_cosine[...]))
+    advanced = wave_exponential(fields, own_kx[:, 0:1], ky[:, :width], (end_sine[...], end_cosine[...]))
     for f in range(3):
         for i in range(2):
-            result[f, i] = advanced[f][i]
+            result[f, i] = advanced[f][i] - state[f, i]
 
     for t in range(chunks):
         give_own(t).wait_send()
@@ -995,47 +1063,24 @@
     chunks = max(1, half // CHUNK_ROWS)
     hb = half // chunks
     dims = (slots, chunks, hb, width, block)
-    g, a = lax.axis_index("space"), lax.axis_index("avg")
-    q, core = a // 2, a % 2
-    low = g < slots // 2
-    phase = phase_index[0].astype(jnp.float32) * phase_step
-    weight = weight_count[0].astype(jnp.float32) / (weight_scale * owners)
-    phase = jnp.where(jnp.arange(128) == 0, phase, weight).reshape(1, 128)
-
-    m, c = jnp.arange(2, dtype=jnp.int32), jnp.arange(2, dtype=jnp.int32)[:, None]
-    order = (2 * ((q + m) % 2) + (core + c) % 2).reshape(-1)
-    columns = (order[:, None] * width + jnp.arange(width, dtype=jnp.int32)).reshape(1, -1)
-    ky = wave_of(columns, length)
-    packed = jnp.asarray(cube_table(length, slots, chunks))
-
-    base = block * jnp.where(low, g, slots - 1 - g) + half * q
-    direct = base + jnp.arange(half, dtype=jnp.int32)
-    mirrored = jnp.where(direct == 0, length // 2, length - direct)
-    begins = jnp.arange(half) == 0
-    zeros = jnp.zeros((half,), jnp.float32)
-    info = jnp.stack([
-        wave_of(direct, length), wave_of(mirrored, length), (direct == 0).astype(jnp.float32),
-        (begins & (q == 0)).astype(jnp.float32), (begins & ~low).astype(jnp.float32),
-        zeros, zeros, zeros,
-    ], axis=1).reshape(chunks, hb, 8)
-    own_kx = wave_of(g * block + jnp.arange(block, dtype=jnp.int32)[:, None], length)
-
-    r = np.arange(block)
-    rows = np.zeros((2, block, block), np.float32)
-    rows[0, r, r] = 1
-    rows[1, r, -r % block] = 1
-    rows = jnp.asarray(rows.astype(ml_dtypes.bfloat16))
-
+    spans = ((1, FINE), (FINE, width // FINE), (width, owners))
+    table = np.concatenate([
+        part for step, count in spans
+        for part in circle(step * np.arange(count)[:, None] * np.arange(length), length)
+    ])
+    table = jnp.asarray(table)
     piece = (3, 2, hb, width)
     dma = pltpu.SemaphoreType.DMA
     vmem = lambda *shape: pltpu.VMEM(shape, jnp.bfloat16)
     wide = lambda *shape: pltpu.VMEM(shape, jnp.float32)
-    return pl.pallas_call(
+    return spectral_state + pl.pallas_call(
         functools.partial(cube_kernel, dims),
         out_shape=jax.ShapeDtypeStruct(spectral_state.shape, jnp.float32),
-        in_specs=[VMEM] * 9 + [pl.BlockSpec(memory_space=pl.ANY)],
+        in_specs=[pl.BlockSpec(memory_space=pltpu.SMEM)] * 2 + [pl.BlockSpec(memory_space=pl.ANY)] * 2,
         out_specs=VMEM,
         scratch_shapes=[
+            wide(3, 2, block, width), vmem(block, block), wide(chunks, hb, 128), wide(1, length),
+            wide(block, 128), wide(*table.shape),
             wide(8, 128), wide(8, 128),
             vmem(2, chunks, *piece), vmem(EDGE, width),
             vmem(chunks, 2, 2, 2, *piece), vmem(2, 2, EDGE, width),
@@ -1058,14 +1103,13 @@
             dma((chunks, slots)), dma((chunks, slots)), dma((chunks,)),
             dma((chunks,)), dma((chunks,)),
             dma((chunks, 3)), dma((chunks, 3)), dma((chunks,)),
-            dma((2,)), dma((2,)), dma(()),
+            dma((2,)), dma((2,)), dma((2,)),
         ],
         compiler_params=pltpu.CompilerParams(
-            collective_id=0, has_side_effects=True, vmem_limit_bytes=56 * 2**20
+            collective_id=0, has_side_effects=True, vmem_limit_bytes=52 * 2**20
         ),
         name="averaged_step",
-    )(spectral_state, rows, info, ky, own_kx, phase,
-      *angle_tables(length, width, owners), packed)
+    )(phase_index, weight_count, spectral_state, table)
 
 
 CHUNK_ROWS = 16

time: 81 us -> 72.3 us (0.89)
  Pallas kernels: 73.9 us -> 67.2 us
  other arithmetic: 2.03 us -> 0.98 us
  local copies, waits for them, and re-layouts: 2.93 us -> 2.09 us
    pallas_call x1, Pallas kernels: 73.9 us -> 67.2 us  [cube_step(): pl.pallas_call(functools.partial(cube_kernel, dims), out_shape=jax.ShapeD...]
    mul x4 -> x0, other arithmetic: 1.41 us -> none  [the longest x3 1.34 us: wave_of(): return shifted.astype(jnp.float32) * (2.0 / length)]
    add x0 -> x1, other arithmetic: none -> 0.98 us  [cube_step(): spectral_state + pl.pallas_call(functools.partial(cube_kernel, dims), out...]
    unnamed x2 -> x4, local copies, waits for them, and re-layouts: 2.11 us -> 2.09 us
where the time goes in v1:
time: 72.3 us; the launch traced here: 71.5 us
  Pallas kernels  67.2 us (93%)
  local copies, waits for them, and re-layouts  2.09 us (3%)
  between operations  1.31 us (2%)
  other arithmetic  0.98 us (1%)
    pallas_call x1, Pallas kernels, cube_step(): pl.pallas_call(functools.partial(cube_kernel, dims), out_shape=jax.ShapeD...  67.2 us
    unnamed x4, local copies, waits for them, and re-layouts  2.09 us

profile of v1, /device:TPU:17, one launch (start us, length us, event | category | flops | bytes accessed | tf_op | source)
XLA Modules:
  0.0 71.5 jit_solution(13347225672120739481)
XLA Ops:
  1.3 0.0 copy-start
  1.3 1.1 %copy-done = f32[3,2,128,256]{3,2,1,0:T(8,128)S(1)} copy-done((f32[3,2,128,256]{3,2,1,0:T(8,128)S(1)}, f32[3,2,128,256]{3,2,1,0:T(8,128)}, u32[]{:S(2)}) %copy-start) | copy-done | bytes 786456
  2.4 0.0 copy-start.1
  2.4 1.0 %copy-done.1 = f32[72,1024]{1,0:T(8,128)S(1)} copy-done((f32[72,1024]{1,0:T(8,128)S(1)}, f32[72,1024]{1,0:T(8,128)}, u32[]{:S(2)}) %copy-start.1) | copy-done | bytes 294936
  3.4 67.2 %averaged_step.1 = f32[3,2,128,256]{3,2,1,0:T(8,128)S(1)} custom-call(s32[1]{0:T(128)S(6)} %copy.5.phase_ref, s32[1]{0:T(128)S(6)} %copy.6.weight_ref, f32[3,2,128,256]{3,2,1,0:T(8,128)S(1)} %copy-done, f32[72,1024]{1,0:T(8,128)S(1)} %copy-done.1), custom_call_target="tpu_custom_call" | custom-call | tf_op jit(solution)/shard_map/averaged_step/pallas_call | solution.py:1076
  70.6 1.0 %add.3 = f32[3,2,128,256]{3,2,1,0:T(8,128)} add(f32[3,2,128,256]{3,2,1,0:T(8,128)S(1)} %copy-done, f32[3,2,128,256]{3,2,1,0:T(8,128)S(1)} %averaged_step.1) | non-fusion elementwise | flops 196608 | bytes 2359296 | tf_op jit(solution)/shard_map/add | solution.py:1076
Async XLA Ops:
  1.3 1.1 %copy-start = (f32[3,2,128,256]{3,2,1,0:T(8,128)S(1)}, f32[3,2,128,256]{3,2,1,0:T(8,128)}, u32[]{:S(2)}) copy-start(f32[3,2,128,256]{3,2,1,0:T(8,128)} %state_hbm.1) | copy-start | bytes 2359300
  2.4 1.0 %copy-start.1 = (f32[72,1024]{1,0:T(8,128)S(1)}, f32[72,1024]{1,0:T(8,128)}, u32[]{:S(2)}) copy-start(f32[72,1024]{1,0:T(8,128)} %constant.2.clone.table_hbm) | copy-start | bytes 884740

commit v2 on v1

--- a/solution.py
+++ b/solution.py
@@ -877,6 +877,11 @@
 
     depth = length // chunks
 
+    def send_rows(t):
+        for d in sending(slots):
+            to_rows(t, d).start()
+        pltpu.make_async_copy(fh.at[t, me], ret.at[t, me], m_s.at[t]).start()
+
     def on_grid(t):
         for d in range(1, slots):
             to_grid(t, d).wait_recv()
@@ -933,9 +938,8 @@
             ).astype(jnp.bfloat16)
             for n in range(256 // (2 * hb)):
                 fh[t, k // (2 * hb) + n] = value[n * 2 * hb : (n + 1) * 2 * hb]
-        for d in sending(slots):
-            to_rows(t, d).start()
-        pltpu.make_async_copy(fh.at[t, me], ret.at[t, me], m_s.at[t]).start()
+        if t < 2:
+            send_rows(t)
 
     def pass_on(t):
         sum_cores(t).wait_recv()
@@ -963,14 +967,18 @@
         for d in range(1, slots):
             to_rows(t, d).wait_recv()
         pltpu.make_async_copy(fh.at[t, me], ret.at[t, me], m_s.at[t]).wait()
+        if t + 2 < chunks:
+            send_rows(t + 2)
         for p in range(slots):
             for k in range(5):
                 lhs[k * 2 * hb : (k + 1) * 2 * hb, p * block : (p + 1) * block] = (
                     ret[t, p, :, k * block : (k + 1) * block]
                 )
         own_pair = column(info, t, 2) > 0.5
-        for j in range(4):
+        for j in (2, 3, 0, 1):
             c, m = divmod(j, 2)
+            if j == 0:
+                sum_cores(t).start()
             span = slice(j * width, (j + 1) * width)
             by_c = lax.dot_general(lhs[...], ct[span, :], DIMS_NT, preferred_element_type=jnp.float32)
             by_s = lax.dot_general(lhs[...], st[span, :], DIMS_NT, preferred_element_type=jnp.float32)
@@ -996,7 +1004,6 @@
                 for f in range(3):
                     for i in range(2):
                         stage[t, c, m, s, f, i] = back[f][i].astype(jnp.bfloat16)
-        sum_cores(t).start()
         pass_on(t)
 
     for t in range(chunks):
@@ -1038,12 +1045,12 @@
             )
             rows = jnp.concatenate(pieces, axis=0).astype(jnp.bfloat16)
             averaged = jnp.dot(order_rows[...], rows, preferred_element_type=jnp.float32)
-            result[f, i] = state[f, i] + time_step * averaged
+            result[f, i] = state[f, i] * (1.0 / time_step) + averaged
     fields = [[result[f, i] for i in range(2)] for f in range(3)]
     advanced = wave_exponential(fields, own_kx[:, 0:1], ky[:, :width], (end_sine[...], end_cosine[...]))
     for f in range(3):
         for i in range(2):
-            result[f, i] = advanced[f][i] - state[f, i]
+            result[f, i] = advanced[f][i]
 
     for t in range(chunks):
         give_own(t).wait_send()
@@ -1073,10 +1080,10 @@
     dma = pltpu.SemaphoreType.DMA
     vmem = lambda *shape: pltpu.VMEM(shape, jnp.bfloat16)
     wide = lambda *shape: pltpu.VMEM(shape, jnp.float32)
-    return spectral_state + pl.pallas_call(
+    return time_step * pl.pallas_call(
         functools.partial(cube_kernel, dims),
         out_shape=jax.ShapeDtypeStruct(spectral_state.shape, jnp.float32),
-        in_specs=[pl.BlockSpec(memory_space=pltpu.SMEM)] * 2 + [pl.BlockSpec(memory_space=pl.ANY)] * 2,
+        in_specs=[pl.BlockSpec(memory_space=pltpu.SMEM)] * 2 + [pl.BlockSpec(memory_space=pltpu.HBM)] * 2,
         out_specs=VMEM,
         scratch_shapes=[
             wide(3, 2, block, width), vmem(block, block), wide(chunks, hb, 128), wide(1, length),
@@ -1106,7 +1113,7 @@
             dma((2,)), dma((2,)), dma((2,)),
         ],
         compiler_params=pltpu.CompilerParams(
-            collective_id=0, has_side_effects=True, vmem_limit_bytes=52 * 2**20
+            collective_id=0, has_side_effects=True, vmem_limit_bytes=105 * 2**19
         ),
         name="averaged_step",
     )(phase_index, weight_count, spectral_state, table)

time: 72.3 us -> 70.8 us (0.979)
  local copies, waits for them, and re-layouts: 2.09 us -> 0.96 us
    unnamed x4 -> x2, local copies, waits for them, and re-layouts: 2.09 us -> 0.96 us
    add x1 -> x0, other arithmetic: 0.98 us -> none  [cube_step(): spectral_state + pl.pallas_call(functools.partial(cube_kernel, dims), out...]
    mul x0 -> x1, other arithmetic: none -> 0.96 us  [cube_step(): time_step * pl.pallas_call(functools.partial(cube_kernel, dims), out_shap...]
where the time goes in v2:
time: 70.8 us; the launch traced here: 70.6 us
  Pallas kernels  67.4 us (95%)
  between operations  1.31 us (2%)
  local copies, waits for them, and re-layouts  0.96 us (1%)
  other arithmetic  0.96 us (1%)
    pallas_call x1, Pallas kernels, cube_step(): pl.pallas_call(functools.partial(cube_kernel, dims), out_shape=jax.ShapeD...  67.4 us

profile of v2, /device:TPU:17, one launch (start us, length us, event | category | flops | bytes accessed | tf_op | source)
XLA Modules:
  0.0 70.6 jit_solution(15169271465513634270)
XLA Ops:
  1.3 0.0 copy-start
  1.3 1.0 %copy-done = f32[72,1024]{1,0:T(8,128)S(1)} copy-done((f32[72,1024]{1,0:T(8,128)S(1)}, f32[72,1024]{1,0:T(8,128)}, u32[]{:S(2)}) %copy-start) | copy-done | bytes 294936
  2.3 67.4 %averaged_step.1 = f32[3,2,128,256]{3,2,1,0:T(8,128)S(1)} custom-call(s32[1]{0:T(128)S(6)} %copy.5.phase_ref, s32[1]{0:T(128)S(6)} %copy.6.weight_ref, f32[3,2,128,256]{3,2,1,0:T(8,128)} %state_hbm.1, f32[72,1024]{1,0:T(8,128)S(1)} %copy-done), custom_call_target="tpu_custom_call" | custom-call | tf_op jit(solution)/shard_map/averaged_step/pallas_call | solution.py:1083
  69.7 1.0 %broadcast_multiply_fusion = f32[3,2,128,256]{3,2,1,0:T(8,128)} fusion(f32[3,2,128,256]{3,2,1,0:T(8,128)S(1)} %averaged_step.1), kind=kLoop, calls=%fused_computation | loop fusion | flops 196608 | bytes 1572864 | tf_op jit(solution)/shard_map/mul | solution.py:1083
Async XLA Ops:
  1.3 1.0 %copy-start = (f32[72,1024]{1,0:T(8,128)S(1)}, f32[72,1024]{1,0:T(8,128)}, u32[]{:S(2)}) copy-start(f32[72,1024]{1,0:T(8,128)} %constant.4.clone.table_hbm) | copy-start | bytes 884740

commit v3 on v2

--- a/solution.py
+++ b/solution.py
@@ -586,7 +586,7 @@
 
 def cube_kernel(
     dims, phase_ref, weight_ref, state_hbm, table_hbm, result,
-    state, order_rows, info, ky, own_kx, parts, ph_mine, ph_got, moved, top, gx, eg, rows_c, rows_s, half, arr, arr_t, grid, products, packed,
+    state, order_rows, order_part, info, ky, own_kx, parts, ph_mine, ph_got, moved, top, gx, eg, rows_c, rows_s, half, arr, arr_t, grid, products, packed,
     ct, st, sine, cosine, end_sine, end_cosine, fh, ret, lhs, stage, rsin, xs, rb, lt, le,
     ph_s, ph_r, x_s, x_r, c_s, c_r, g_s, eg_s, eg_r, a_s, a_r, l_s,
     b_s, b_r, m_s, d_s, d_r, y_s, y_r, k_s, le_s, le_r, load_s,
@@ -659,6 +659,12 @@
     order_rows[...] = jnp.where(
         along == down + side * (turned_down - down), 1.0, 0.0
     ).astype(jnp.bfloat16)
+    down = lax.broadcasted_iota(jnp.int32, (block, 2 * hb), 0)
+    along = lax.broadcasted_iota(jnp.int32, (block, 2 * hb), 1)
+    moved_down = down + side * (jnp.where(down == 0, 0, block - down) - down)
+    for t in range(chunks):
+        spot = along + t * hb + (along // hb) * (reach - hb)
+        order_part[t] = jnp.where(spot == moved_down, 1.0, 0.0).astype(jnp.bfloat16)
     lane = lax.broadcasted_iota(jnp.int32, ph_mine.shape, 1)
     ph_mine[...] = jnp.where(
         lane == 0, phase_ref[0].astype(jnp.float32) * phase_step,
@@ -938,8 +944,10 @@
             ).astype(jnp.bfloat16)
             for n in range(256 // (2 * hb)):
                 fh[t, k // (2 * hb) + n] = value[n * 2 * hb : (n + 1) * 2 * hb]
-        if t < 2:
-            send_rows(t)
+        if t == 0:
+            send_rows(0)
+        if t == min(2, chunks - 1) and chunks > 1:
+            send_rows(1)
 
     def pass_on(t):
         sum_cores(t).wait_recv()
@@ -953,7 +961,6 @@
                         for i in range(2):
                             tile = tile + only_row(2 * f + i, value[f, i, 0:1], EDGE)
                     lt[m] = tile.astype(jnp.bfloat16)
-        for m in range(2):
             give_mirror(t, m).start()
         give_own(t).start()
         give_self(t).start()
@@ -1026,26 +1033,31 @@
         for k in range(2):
             remote(lt.at[0], le.at[k], le_s.at[0], le_r.at[k], g, partner).wait_recv()
 
+    edge = le[0].astype(jnp.float32) + le[1].astype(jnp.float32)
+    for f in range(3):
+        for i in range(2):
+            result[f, i] = state[f, i] * (1.0 / time_step)
     for t in range(chunks):
         give_own(t).wait_recv()
         for m in range(2):
             give_mirror(t, m).wait_recv()
         give_self(t).wait()
-
-    edge = le[0].astype(jnp.float32) + le[1].astype(jnp.float32)
-    for f in range(3):
-        for i in range(2):
-            pieces = [
-                rb[t, 0, h, f, i].astype(jnp.float32) + rb[t, 1, h, f, i].astype(jnp.float32)
-                for h in range(2) for t in range(chunks)
-            ]
-            n = 2 * f + i
-            pieces[0] = jnp.where(
-                column(info, 0, 4) > 0.5, jnp.broadcast_to(edge[n : n + 1], (hb, width)), pieces[0]
-            )
-            rows = jnp.concatenate(pieces, axis=0).astype(jnp.bfloat16)
-            averaged = jnp.dot(order_rows[...], rows, preferred_element_type=jnp.float32)
-            result[f, i] = state[f, i] * (1.0 / time_step) + averaged
+        for f in range(3):
+            for i in range(2):
+                pieces = [
+                    rb[t, 0, h, f, i].astype(jnp.float32) + rb[t, 1, h, f, i].astype(jnp.float32)
+                    for h in range(2)
+                ]
+                n = 2 * f + i
+                if t == 0:
+                    pieces[0] = jnp.where(
+                        column(info, 0, 4) > 0.5, jnp.broadcast_to(edge[n : n + 1], (hb, width)), pieces[0]
+                    )
+                rows = jnp.concatenate(pieces, axis=0).astype(jnp.bfloat16)
+                averaged = jnp.dot(
+                    order_part[t], rows, preferred_element_type=jnp.float32
+                )
+                result[f, i] = result[f, i] + averaged
     fields = [[result[f, i] for i in range(2)] for f in range(3)]
     advanced = wave_exponential(fields, own_kx[:, 0:1], ky[:, :width], (end_sine[...], end_cosine[...]))
     for f in range(3):
@@ -1086,7 +1098,7 @@
         in_specs=[pl.BlockSpec(memory_space=pltpu.SMEM)] * 2 + [pl.BlockSpec(memory_space=pltpu.HBM)] * 2,
         out_specs=VMEM,
         scratch_shapes=[
-            wide(3, 2, block, width), vmem(block, block), wide(chunks, hb, 128), wide(1, length),
+            wide(3, 2, block, width), vmem(block, block), vmem(chunks, block, 2 * hb), wide(chunks, hb, 128), wide(1, length),
             wide(block, 128), wide(*table.shape),
             wide(8, 128), wide(8, 128),
             vmem(2, chunks, *piece), vmem(EDGE, width),

time: 70.8 us -> 70.7 us (level)
  no operation moved by 1% of the time
where the time goes in v3:
time: 70.7 us; the launch traced here: 70.5 us
  Pallas kernels  67.3 us (95%)
  between operations  1.31 us (2%)
  local copies, waits for them, and re-layouts  0.96 us (1%)
  other arithmetic  0.96 us (1%)
    pallas_call x1, Pallas kernels, cube_step(): pl.pallas_call(functools.partial(cube_kernel, dims), out_shape=jax.ShapeD...  67.3 us

profile of v3, /device:TPU:17, one launch (start us, length us, event | category | flops | bytes accessed | tf_op | source)
XLA Modules:
  0.0 70.5 jit_solution(6342675875814094298)
XLA Ops:
  1.3 0.0 copy-start
  1.3 1.0 %copy-done = f32[72,1024]{1,0:T(8,128)S(1)} copy-done((f32[72,1024]{1,0:T(8,128)S(1)}, f32[72,1024]{1,0:T(8,128)}, u32[]{:S(2)}) %copy-start) | copy-done | bytes 294936
  2.3 67.3 %averaged_step.1 = f32[3,2,128,256]{3,2,1,0:T(8,128)S(1)} custom-call(s32[1]{0:T(128)S(6)} %copy.5.phase_ref, s32[1]{0:T(128)S(6)} %copy.6.weight_ref, f32[3,2,128,256]{3,2,1,0:T(8,128)} %state_hbm.1, f32[72,1024]{1,0:T(8,128)S(1)} %copy-done), custom_call_target="tpu_custom_call" | custom-call | tf_op jit(solution)/shard_map/averaged_step/pallas_call | solution.py:1095
  69.5 1.0 %broadcast_multiply_fusion = f32[3,2,128,256]{3,2,1,0:T(8,128)} fusion(f32[3,2,128,256]{3,2,1,0:T(8,128)S(1)} %averaged_step.1), kind=kLoop, calls=%fused_computation | loop fusion | flops 196608 | bytes 1572864 | tf_op jit(solution)/shard_map/mul | solution.py:1095
Async XLA Ops:
  1.3 1.0 %copy-start = (f32[72,1024]{1,0:T(8,128)S(1)}, f32[72,1024]{1,0:T(8,128)}, u32[]{:S(2)}) copy-start(f32[72,1024]{1,0:T(8,128)} %constant.4.clone.table_hbm) | copy-start | bytes 884740
